TPU v7x, 32 devices: a whole 2x2x4 slice. The times are simulated.
32 devices in a mesh: study: 2 (over x), vol: 8 (over z, y), tile: 2 (over core).
Axes of the slice: x: 2, y: 2, z: 4, core: 2. Of those that a mesh axis runs over, the one named last changes fastest.
Arguments:
- spectra: bfloat16 [16, 4, 768, 2048], P(('study', 'vol'), None, 'tile'), parts along dimension 0, may hold values from -6 to 6
- block_scales: float32 [16, 4, 768, 16], P(('study', 'vol'), None, 'tile'), parts along dimension 0, may hold values from 0.3 to 3
- retina_blocks: int32 [12, 2], P(('study', 'tile')), parts along dimension 0, may hold values from 0 to 3, as said below
- quality_block: int32 [16, 6], P(('study', 'vol'), 'tile'), parts along dimension 0, may hold values from 0 to 3, as said below
- quality_bias: float32 [16, 6], P(('study', 'vol'), 'tile'), parts along dimension 0, may hold values from -110 to 160
Outputs:
- angiogram: float32 [1024, 768], P(('study', 'vol'), 'tile'), parts along dimension 0
- joined_structure: float32 [1024, 768], P(('study', 'vol'), 'tile'), parts along dimension 0
- spread_map: float32 [1024, 768], P(('study', 'vol'), 'tile'), parts along dimension 0
There are 2 independent parts, one for each index of `study`. A program takes and returns all parts, laid end to end along the dimension named above; each array names one. Nothing has to cross between parts.
Inputs may be any that keep to these rules, and one draw needn't show every extreme that they name: retina_blocks[j,0] <= retina_blocks[j,1]. quality_block[v,j] lies between retina_blocks[j,0] and retina_blocks[j,1].
All inputs are finite; a program needn't handle non-finite values.
Results may differ from a plain program's by a relative error of at most 0.0015.
Values sent between devices are 32-bit elements; how exact they have to be, the bound alone decides.
A program may use at most 128 MiB of HBM per device.

v0:
```python
import math

import jax
import jax.numpy as jnp
from jax import lax
from jax.sharding import PartitionSpec as P

K = 2048
DEPTH = 512
BANDS = 4
REPEATS = 4
DBLK = 128
ABLK = 128
SB = 128
NDB = 4


smooth_taps = (1.0 / 9.0, 2.0 / 9.0, 3.0 / 9.0, 2.0 / 9.0, 1.0 / 9.0)


def padded_2(array, sides, width):
    for axis, dim in sides:
        count, length = (lax.axis_size(axis), array.shape[dim])
        up = [(i, (i + 1) % count) for i in range(count - 1)]
        down = [(j, i) for i, j in up]
        last = lax.slice_in_dim(array, length - width, length, axis=dim)
        initial = lax.slice_in_dim(array, 0, width, axis=dim)
        before = lax.ppermute(last, axis, up)
        after = lax.ppermute(initial, axis, down)
        array = jnp.concatenate([before, array, after], axis=dim)
    return array


def window_tables():
    sample_index = jnp.arange(K, dtype=jnp.int32)
    depth_index = jnp.arange(DEPTH, dtype=jnp.int32)
    phase_angle = (sample_index[:, None] * depth_index[None, :] % K).astype(jnp.float32) * (
        2.0 * math.pi / K
    )
    kernel = jnp.stack([jnp.cos(phase_angle), -jnp.sin(phase_angle)], axis=1)
    centres = (jnp.arange(BANDS, dtype=jnp.float32)[:, None] + 0.5) * (K / BANDS)
    distance = sample_index.astype(jnp.float32)[None, :] - centres
    offsets = distance / (K / 8.0)
    window = jnp.where(jnp.abs(distance) <= K / 2.0, jnp.exp(-0.5 * offsets * offsets), 0.0)
    window = window / jnp.sqrt(jnp.sum(window * window, axis=1, keepdims=True))
    return (window[:, :, None, None] * kernel[None]).astype(jnp.bfloat16)


def spread_columns(values, repeat_width):
    widened = jnp.broadcast_to(values[..., None], values.shape + (repeat_width,))
    return widened.reshape(values.shape[:-1] + (values.shape[-1] * repeat_width,))


def scale_spectra(spectra_vol, scales_vol):
    shaped = spectra_vol.astype(jnp.float32).reshape(scales_vol.shape + (SB,))
    return (shaped * scales_vol[..., None]).reshape(spectra_vol.shape).astype(jnp.bfloat16)


def band_maps(scaled, tables):
    line_count = scaled.shape[1]
    decorrelation = jnp.zeros((DEPTH, line_count), jnp.float32)
    power_total = jnp.zeros((DEPTH, line_count), jnp.float32)
    for band_index in range(BANDS):
        fields = jnp.einsum(
            "kcd,rak->cdra", tables[band_index], scaled, preferred_element_type=jnp.float32
        )
        band_power = fields[0] * fields[0] + fields[1] * fields[1]
        amplitude = jnp.sqrt(band_power + 0.05)
        pair_ratio = (
            2.0
            * amplitude[:, :-1]
            * amplitude[:, 1:]
            / (band_power[:, :-1] + band_power[:, 1:] + 0.1)
        )
        decorrelation = decorrelation + jnp.sum(1.0 - pair_ratio, axis=1)
        power_total = power_total + jnp.sum(band_power, axis=1)
    decorrelation = decorrelation / (BANDS * (REPEATS - 1))
    structure = jnp.log(power_total / (BANDS * REPEATS) + 0.1)
    return (decorrelation, structure)


def retina_mask(first_col, last_col):
    depth_block = jnp.arange(DEPTH, dtype=jnp.int32) // DBLK
    return (depth_block[:, None] >= first_col[None, :]) & (
        depth_block[:, None] <= last_col[None, :]
    )


def lateral_smooth(padded, line_count):
    filtered = smooth_taps[0] * padded[:, 0:line_count]
    for offset_index in range(1, 5):
        filtered = (
            filtered
            + smooth_taps[offset_index] * padded[:, offset_index : offset_index + line_count]
        )
    return filtered


def block_quality(structure, qblock):
    tile_count = qblock.shape[0]
    block_means = jnp.mean(structure.reshape(NDB, DBLK, tile_count, ABLK), axis=(1, 3))
    chosen = jnp.arange(NDB, dtype=jnp.int32)[:, None] == qblock[None, :]
    return jnp.sum(jnp.where(chosen, block_means, 0.0), axis=0)


def on_device(spectra, block_scales, retina_blocks, quality_block, quality_bias):
    tables = window_tables()
    scaled = scale_spectra(spectra[0], block_scales[0])
    line_count = scaled.shape[1]
    decorrelation, structure = band_maps(scaled, tables)
    first_col = spread_columns(retina_blocks[:, 0], ABLK)
    last_col = spread_columns(retina_blocks[:, 1], ABLK)
    inside = retina_mask(first_col, last_col)
    masked_decorrelation = jnp.where(inside, decorrelation, 0.0)
    masked_structure = jnp.where(inside, structure, 0.0)
    padded = padded_2(masked_decorrelation, (("tile", 1),), 2)
    smoothed = lateral_smooth(padded, line_count)
    volume_score = block_quality(structure, quality_block[0]) + quality_bias[0]
    scores = lax.all_gather(volume_score[None, :], "vol", axis=0, tiled=True)
    top_score = jnp.max(scores, axis=0)
    weight_total = jnp.sum(jnp.exp(scores - top_score[None, :]), axis=0)
    own_weight = spread_columns(jnp.exp(volume_score - top_score) / weight_total, ABLK)[None, :]
    stacked = jnp.stack(
        [own_weight * smoothed, own_weight * smoothed * smoothed, own_weight * masked_structure]
    )
    joined_maps = lax.psum_scatter(stacked, "vol", scatter_dimension=1, tiled=True)
    angiogram = joined_maps[0]
    second_moment = joined_maps[1]
    joined_structure = joined_maps[2]
    spread_map = jnp.sqrt(second_moment - angiogram * angiogram + 0.01)
    return (angiogram, joined_structure, spread_map)


def solution(mesh):
    return jax.shard_map(
        on_device,
        mesh=mesh,
        in_specs=(
            P(("study", "vol"), None, "tile", None),
            P(("study", "vol"), None, "tile", None),
            P(("study", "tile"), None),
            P(("study", "vol"), "tile"),
            P(("study", "vol"), "tile"),
        ),
        out_specs=(
            P(("study", "vol"), "tile"),
            P(("study", "vol"), "tile"),
            P(("study", "vol"), "tile"),
        ),
        check_vma=False,
    )
```

profile of v0, /device:TPU:13, one launch (start us, length us, event | category | flops | bytes accessed | tf_op | source)
XLA Modules:
  0.0 230.5 jit_solution(10307218010125406644)
XLA Ops:
  7.2 0.0 reduce-scatter.2.cloned.1.call-start
  7.2 0.0 copy-start
  7.3 17.7 %sine_negate_fusion = (f32[2048,1,512]{0,2,1:T(8,128)}, f32[2048,1,512]{0,2,1:T(8,128)}) fusion(), kind=kLoop, calls=%fused_computation.18 | loop fusion | flops 15728640 | bytes 8388608 | tf_op jit(solution)/shard_map/neg | solution.py:40
  24.9 0.2 multiply_reduce_fusion
  25.2 0.1 broadcast_divide_fusion
  25.3 0.0 copy-done
  25.3 0.3 copy.13
  25.5 5.0 %copy.20 = f32[192,8,16,128]{3,2,1,0:T(8,128)S(1)} copy(bf16[192,8,16,128]{3,1,2,0:T(8,128)(2,1)} %bitcast.110) | data formatting | bytes 18874368
  30.6 5.9 %fusion = bf16[4,384,16,128]{3,2,1,0:T(8,128)(2,1)} fusion(f32[4,384,16]{2,1,0:T(8,128)S(1)} %copy.13, f32[4,384,16,128]{3,2,1,0:T(8,128)S(1)} %bitcast.107), kind=kLoop, calls=%fused_computation.2 | loop fusion | flops 6291456 | bytes 18972672 | tf_op jit(solution)/shard_map/convert_element_type | solution.py:56
  36.5 10.3 %reshape.414 = bf16[4,384,2048,1]{2,1,0,3:T(8,128)(2,1)} reshape(bf16[4,384,16,128]{3,2,1,0:T(8,128)(2,1)} %fusion) | data formatting | bytes 12582912 | tf_op jit(solution)/shard_map/convert_element_type | solution.py:56
  46.8 0.0 slice-start
  46.8 4.2 %pad_maximum_fusion = f32[2048,2,512]{0,2,1:T(8,128)S(1)} fusion(f32[2048,1,512]{0,2,1:T(8,128)} %get-tuple-element.19, f32[2048,1,512]{0,2,1:T(8,128)} %get-tuple-element.20), kind=kLoop, calls=%fused_computation.3 | loop fusion | flops 2097152 | bytes 16777216 | tf_op jit(solution)/shard_map/stack | solution.py:40
  51.0 0.0 slice-start.1
  51.0 6.3 %multiply_convert_fusion = bf16[4,2048,2,512]{1,3,2,0:T(8,128)(2,1)} fusion(f32[2048,2,512]{0,2,1:T(8,128)S(1)} %pad_maximum_fusion, f32[4,2048]{1,0:T(4,128)S(1)} %broadcast_divide_fusion), kind=kLoop, calls=%fused_computation | loop fusion | flops 16777216 | bytes 25198592 | tf_op jit(solution)/shard_map/convert_element_type | solution.py:46
  57.3 0.0 slice-done
  57.3 0.0 slice-done.1
  57.3 8.5 %fusion.4 = f32[2,512,4,384]{3,1,2,0:T(8,128)S(1)} fusion(bf16[4,384,2048,1]{2,1,0,3:T(8,128)(2,1)S(1)} %bitcast.109, bf16[4,2048,2,512]{1,3,2,0:T(8,128)(2,1)} %multiply_convert_fusion), kind=kOutput, calls=%fused_computation.11 | convolution fusion | flops 6442450944 | bytes 16777216 | tf_op jit(solution)/shard_map/kcd,rak->cdra/dot_general | solution.py:64
  65.9 8.6 %fusion.5 = f32[2,512,4,384]{3,1,2,0:T(8,128)S(1)} fusion(bf16[4,384,2048,1]{2,1,0,3:T(8,128)(2,1)S(1)} %bitcast.109, bf16[4,2048,2,512]{1,3,2,0:T(8,128)(2,1)} %multiply_convert_fusion), kind=kOutput, calls=%fused_computation.13 | convolution fusion | flops 6442450944 | bytes 16777216 | tf_op jit(solution)/shard_map/kcd,rak->cdra/dot_general | solution.py:64
  74.4 8.7 %fusion.6 = f32[2,512,4,384]{3,1,2,0:T(8,128)S(1)} fusion(bf16[4,384,2048,1]{2,1,0,3:T(8,128)(2,1)S(1)} %bitcast.109, bf16[4,2048,2,512]{1,3,2,0:T(8,128)(2,1)} %multiply_convert_fusion), kind=kOutput, calls=%fused_computation.15 | convolution fusion | flops 6442450944 | bytes 16777216 | tf_op jit(solution)/shard_map/kcd,rak->cdra/dot_general | solution.py:64
  83.2 0.0 copy-start.1
  83.2 10.3 %fusion.7 = f32[2,512,4,384]{3,1,2,0:T(8,128)S(1)} fusion(bf16[4,384,2048,1]{2,1,0,3:T(8,128)(2,1)} %reshape.414, bf16[4,2048,2,512]{1,3,2,0:T(8,128)(2,1)} %multiply_convert_fusion), kind=kOutput, calls=%fused_computation.17 | convolution fusion | flops 6442450944 | bytes 16777216 | tf_op jit(solution)/shard_map/kcd,rak->cdra/dot_general | solution.py:64
  93.5 0.0 copy-done.1
  93.5 3.8 %add_sqrt_fusion = (f32[512,4,384]{2,0,1:T(8,128)}, f32[512,4,384]{2,0,1:T(8,128)}) fusion(f32[2,512,4,384]{3,1,2,0:T(8,128)S(1)} %fusion.4), kind=kLoop, calls=%fused_computation.34 | loop fusion | flops 3145728 | bytes 12582912 | tf_op jit(solution)/shard_map/sqrt | solution.py:68
  97.3 3.8 %add_sqrt_fusion.1 = (f32[512,4,384]{2,0,1:T(8,128)}, f32[512,4,384]{2,0,1:T(8,128)}) fusion(f32[2,512,4,384]{3,1,2,0:T(8,128)S(1)} %fusion.5), kind=kLoop, calls=%fused_computation.35 | loop fusion | flops 3145728 | bytes 12582912 | tf_op jit(solution)/shard_map/sqrt | solution.py:68
  101.1 3.7 %add_sqrt_fusion.3 = (f32[512,4,384]{2,0,1:T(8,128)}, f32[512,4,384]{2,0,1:T(8,128)}) fusion(f32[2,512,4,384]{3,1,2,0:T(8,128)S(1)} %fusion.7), kind=kLoop, calls=%fused_computation.37 | loop fusion | flops 3145728 | bytes 12582912 | tf_op jit(solution)/shard_map/sqrt | solution.py:68
  104.8 1.1 add_sqrt_fusion.2
  105.9 0.1 broadcast_bitcast_fusion
  106.0 4.7 %fusion.30 = f32[512,384]{1,0:T(8,128)S(1)} fusion(f32[512,4,384]{2,0,1:T(8,128)} %get-tuple-element.14, f32[512,4,384]{2,0,1:T(8,128)} %get-tuple-element.13), kind=kLoop, calls=%fused_computation.66 | loop fusion | flops 3932160 | bytes 10223616 | tf_op jit(solution)/shard_map/reduce_sum | solution.py:75
  110.7 4.7 %fusion.29 = f32[512,384]{1,0:T(8,128)S(1)} fusion(f32[512,4,384]{2,0,1:T(8,128)} %get-tuple-element.12, f32[512,4,384]{2,0,1:T(8,128)} %get-tuple-element.11), kind=kLoop, calls=%fused_computation.65 | loop fusion | flops 3932160 | bytes 10223616 | tf_op jit(solution)/shard_map/reduce_sum | solution.py:75
  115.4 5.5 %fusion.27 = f32[512,384]{1,0:T(8,128)} fusion(f32[512,4,384]{2,0,1:T(8,128)} %get-tuple-element.10, f32[512,4,384]{2,0,1:T(8,128)} %get-tuple-element.9), kind=kLoop, calls=%fused_computation.63 | loop fusion | flops 3932160 | bytes 10223616 | tf_op jit(solution)/shard_map/reduce_sum | solution.py:75
  120.9 1.6 fusion.28
  122.5 1.7 multiply_select_fusion
  124.2 0.9 fusion.73
  125.0 1.3 collective-permute-start
  126.3 0.5 fusion.51
  126.8 0.5 fusion.49
  127.3 0.5 fusion.45
  127.7 0.5 fusion.47
  128.2 0.0 copy-start.3
  128.2 0.0 copy-start.2
  128.2 0.3 add_log_fusion
  128.5 0.3 copy.14
  128.8 0.3 reshape.409
  129.0 0.2 reduce_sum.115
  129.3 0.0 copy-done.3
  129.3 0.2 select_reduce_fusion
  129.5 0.0 copy-done.2
  129.5 3.1 %collective-permute-start.1 = (f32[512,2]{1,0:T(8,128)}, f32[512,2]{1,0:T(8,128)S(1)}, u32[]{:S(2)}, u32[]{:S(2)}) collective-permute-start(f32[512,2]{1,0:T(8,128)} %get-tuple-element.16), channel_id=1, source_target_pairs={{1,0},{3,2},{5,4},{7,6},{9,8},{11,10},{13,12},{15,14},{17,16},{19,... | collective-permute-start | bytes 12296 | tf_op jit(solution)/shard_map/ppermute | solution.py:29
  132.5 10.5 %all-gather = f32[8,1,3]{2,1,0:T(1,128)S(1)} all-gather(f32[1,1,3]{2,1,0:T(1,128)S(1)} %fusion.64), channel_id=1, replica_groups=mesh['study'=2,'vol'=8,'tile'=2] {'vol'}, dimensions={0}, use_global_device_ids=true | all-gather | bytes 108 | tf_op jit(solution)/shard_map/all_gather | solution.py:119
  143.1 0.1 copy.15
  143.2 0.2 fusion.62
  143.4 0.1 broadcast_bitcast_fusion.2
  143.5 0.2 fusion.43
  143.7 0.0 collective-permute-done
  143.7 0.0 collective-permute-done.1
  143.7 1.1 multiply_bitcast_fusion
  144.8 0.1 fusion.40
  144.9 1.6 pad_maximum_fusion.1
  146.4 0.0 reduce-scatter.2.cloned.1.call-update
  146.5 74.0 %reduce-scatter.2.cloned.1.call-done = f32[3,64,384]{2,1,0:T(8,128)} async-done(((f32[3,512,384]{2,1,0:T(8,128)}), f32[3,64,384]{2,1,0:T(8,128)}) %reduce-scatter.2.cloned.1.call-update) | async-done | bytes 294928 | tf_op jit(solution)/shard_map/reduce_scatter | solution.py:126
  220.4 1.5 slice_bitcast_fusion.9
  222.0 1.6 fusion.54
  (9 shorter events, 0.1 us)
Async XLA Ops:
  7.2 213.3 %reduce-scatter.2.cloned.1.call-start = ((), (), s32[]{:S(2)}) async-start(), calls=%async_computation.1 | async-start | bytes 2654208 | tf_op jit(solution)/shard_map/reduce_scatter | solution.py:126
  7.2 18.0 %copy-start = (f32[1,4,384,16]{2,3,1,0:T(8,128)S(1)}, f32[1,4,384,16]{2,3,1,0:T(8,128)}, u32[]{:S(2)}) copy-start(f32[1,4,384,16]{2,3,1,0:T(8,128)} %param.6) | copy-start | bytes 294916
  46.8 10.5 %slice-start = ((s8[6291456]{0:T(1024)(128)(4,1)}), s8[4194304]{0:T(1024)(128)(4,1)S(1)}, s32[]{:S(2)}) async-start(s8[6291456]{0:T(1024)(128)(4,1)} %bitcast.108), calls=%async_computation.2 | async-start | bytes 8388608
  51.0 6.3 %slice-start.1 = ((s8[6291456]{0:T(1024)(128)(4,1)}), s8[2097152]{0:T(1024)(128)(4,1)S(1)}, s32[]{:S(2)}) async-start(s8[6291456]{0:T(1024)(128)(4,1)} %bitcast.108), calls=%async_computation.3 | async-start | bytes 4194304
  83.2 10.3 %copy-start.1 = (s32[3,2]{0,1:T(2,128)S(1)}, s32[3,2]{0,1:T(2,128)}, u32[]{:S(2)}) copy-start(s32[3,2]{0,1:T(2,128)} %param.7) | copy-start | bytes 76
  125.0 18.7 %collective-permute-start = (f32[512,2]{1,0:T(8,128)}, f32[512,2]{1,0:T(8,128)S(1)}, u32[]{:S(2)}, u32[]{:S(2)}) collective-permute-start(f32[512,2]{1,0:T(8,128)} %get-tuple-element.15), channel_id=1, source_target_pairs={{0,1},{2,3},{4,5},{6,7},{8,9},{10,11},{12,13},{14,15},{16,17},{18,... | collective-permute-start | bytes 12296 | tf_op jit(solution)/shard_map/ppermute | solution.py:28
  128.2 1.1 copy-start.3
  128.2 1.3 copy-start.2
  129.5 14.2 %collective-permute-start.1 = (f32[512,2]{1,0:T(8,128)}, f32[512,2]{1,0:T(8,128)S(1)}, u32[]{:S(2)}, u32[]{:S(2)}) collective-permute-start(f32[512,2]{1,0:T(8,128)} %get-tuple-element.16), channel_id=1, source_target_pairs={{1,0},{3,2},{5,4},{7,6},{9,8},{11,10},{13,12},{15,14},{17,16},{19,... | collective-permute-start | bytes 12296 | tf_op jit(solution)/shard_map/ppermute | solution.py:29
Sparse Core Ops, SparseCore 0:
  146.6 73.8 reduce-scatter.1
where the time goes:
time: 235 us; the launch traced here: 230 us
  waiting for transfers between devices  74 us (31%)
  other arithmetic  72.3 us (31%)
  matrix products  36.1 us (15%)
  local copies, waits for them, and re-layouts  18.8 us (8%)
  between operations  14.3 us (6%)
  blocking collectives  10.5 us (4%)
  starting transfers between devices  4.37 us (2%)
    reduce_scatter x1, waiting for transfers between devices, on_device(): lax.psum_scatter(stacked, 'vol', scatter_dimension=1, tiled=True)  74 us
    dot_general x4, matrix products, band_maps(): jnp.einsum('kcd,rak->cdra', tables[band_index], scaled, preferred_element...  36.1 us
    neg x1, other arithmetic, window_tables(): kernel = jnp.stack([jnp.cos(phase_angle), -jnp.sin(phase_angle)], axis=1)  17.7 us
    reduce_sum x4, other arithmetic, band_maps(): decorrelation = decorrelation + jnp.sum(1.0 - pair_ratio, axis=1)  16.5 us
    sqrt x4, other arithmetic, band_maps(): amplitude = jnp.sqrt(band_power + 0.05)  12.5 us
    all_gather x1, blocking collectives, on_device(): scores = lax.all_gather(volume_score[None, :], 'vol', axis=0, tiled=True)  10.5 us
    convert_element_type x1, local copies, waits for them, and re-layouts, scale_spectra(): (shaped * scales_vol[..., None]).reshape(spectra_vol.shape)  10.3 us
    convert_element_type x1, other arithmetic, window_tables(): return (window[:, :, None, None] * kernel[None]).astype(jnp.bfloat16)  6.29 us
  transfers between devices with their start and end apart: 3, of which 1 were waited for; matrix products, arithmetic and copies ran while one was open for 2% of the time, Pallas kernels for 0%

commit v1 on v0

v1 whole, which is shorter than its diff:
```python
import functools
import math

import jax
import jax.numpy as jnp
from jax import lax
from jax.experimental import pallas as pl
from jax.experimental.pallas import tpu as pltpu
from jax.sharding import PartitionSpec as P

DEPTH = 512
BANDS = 4
DBLK = 128
ABLK = 128
SB = 128
NDB = 4
CLASSES = 8
MESH = pl.DeviceIdType.MESH
ZR = 136


def build_tables(table, perm, samples):
    inner = samples // CLASSES
    z = lax.broadcasted_iota(jnp.int32, (ZR, inner), 0)
    k1 = lax.broadcasted_iota(jnp.int32, (ZR, inner), 1)
    unit = 2.0 * math.pi / samples
    base = ((CLASSES * k1 * z) % samples).astype(jnp.float32) * unit
    step = z.astype(jnp.float32) * unit
    re, im = jnp.cos(base), -jnp.sin(base)
    sre, sim = jnp.cos(step), -jnp.sin(step)
    kk = (
        lax.broadcasted_iota(jnp.int32, (CLASSES, inner), 1) * CLASSES
        + lax.broadcasted_iota(jnp.int32, (CLASSES, inner), 0)
    ).astype(jnp.float32)
    windows = []
    for b in range(BANDS):
        distance = kk - (b + 0.5) * (samples / BANDS)
        offset = distance / (samples / 8.0)
        g = jnp.where(jnp.abs(distance) <= samples / 2.0, jnp.exp(-0.5 * offset * offset), 0.0)
        windows.append(g / jnp.sqrt(jnp.sum(g * g, keepdims=True)))
    for k0 in range(CLASSES):
        if k0:
            re, im = re * sre - im * sim, re * sim + im * sre
        both = jnp.concatenate([re, im], axis=0)
        for b in range(BANDS):
            row = windows[b][k0 : k0 + 1, :]
            table[k0, b * 2 * ZR : (b + 1) * 2 * ZR, :] = (both * row).astype(jnp.bfloat16)
    size = perm.shape[0]
    part = size // CLASSES
    row = lax.broadcasted_iota(jnp.int32, (size, size), 0)
    col = lax.broadcasted_iota(jnp.int32, (size, size), 1)
    perm[...] = jnp.where(col == (row % part) * CLASSES + row // part, 1.0, 0.0).astype(jnp.bfloat16)


def combine(get):
    rr, ii = [get(k, 0) for k in range(8)], [get(k, 1) for k in range(8)]
    sr = [rr[j] + rr[j + 4] for j in range(4)]
    si = [ii[j] + ii[j + 4] for j in range(4)]
    dr = [rr[j] - rr[j + 4] for j in range(4)]
    di = [ii[j] - ii[j + 4] for j in range(4)]
    half = math.sqrt(0.5)
    re0, im0 = (sr[0] + sr[2]) + (sr[1] + sr[3]), (si[0] + si[2]) + (si[1] + si[3])
    re3, im3 = (sr[0] - sr[2]) - (si[1] - si[3]), (si[0] - si[2]) + (sr[1] - sr[3])
    p, q = (dr[1] - dr[3]) * half, (di[1] + di[3]) * half
    r, t = (di[1] - di[3]) * half, (dr[1] + dr[3]) * half
    re2, im2 = (dr[0] + di[2]) + (p + q), (di[0] - dr[2]) + (r - t)
    re1, im1 = (dr[0] - di[2]) + (p - q), (di[0] + dr[2]) + (r + t)
    fields = ((re0, im0), (re1, im1), (re2, im2), (re3, im3))
    return [re * re + (im * im + 0.05) for re, im in fields]


def compute_kernel(
    retina, qblock, bias, spec, scales, dec_out, str_out, score_out,
    table, perm, data, ga, gb, acc_ratio, acc_power,
):
    j = pl.program_id(0)
    repeats, lines, samples = spec.shape[1:]
    chunk = perm.shape[0]
    part = chunk // CLASSES
    cols = repeats * lines

    @pl.when(j == 0)
    def _():
        build_tables(table, perm, samples)

    scale_t = jnp.concatenate([scales[0, r].T for r in range(repeats)], axis=1)
    for q in range(samples // chunk):
        block = spec[0, :, :, q * chunk : (q + 1) * chunk].reshape(cols, chunk)
        moved = lax.dot_general(
            perm[...], block, (((1,), (1,)), ((), ())), preferred_element_type=jnp.float32
        )
        per = chunk // SB
        factor = jnp.concatenate(
            [
                jnp.broadcast_to(scale_t[q * per + h : q * per + h + 1, :], (part // per, cols))
                for h in range(per)
            ],
            axis=0,
        )
        for k0 in range(CLASSES):
            data[k0, q * part : (q + 1) * part, :] = (
                moved[k0 * part : (k0 + 1) * part] * factor
            ).astype(jnp.bfloat16)

    buffers = (ga, gb)

    def multiply(b):
        for k0 in range(CLASSES):
            buffers[b % 2][k0] = jnp.dot(
                table[k0, b * 2 * ZR : (b + 1) * 2 * ZR, :],
                data[k0],
                preferred_element_type=jnp.float32,
            )

    def reduce(b):
        g = buffers[b % 2]

        for i in range(ZR // 8):
            at = i * 8
            powers = []
            for r in range(repeats):
                def get(k, c):
                    return g[k, c * ZR + at : c * ZR + at + 8, r * lines : (r + 1) * lines]

                powers.append(combine(get))
            for d in range(NDB):
                total = powers[0][d]
                ratio = None
                for r in range(repeats - 1):
                    first, second = powers[r][d], powers[r + 1][d]
                    total = total + second
                    prod, both = first * second, first + second
                    term = prod * lax.rsqrt(prod * (both * both))
                    ratio = term if ratio is None else ratio + term
                if b:
                    total = total + acc_power[d, at : at + 8, :]
                    ratio = ratio + acc_ratio[d, at : at + 8, :]
                acc_power[d, at : at + 8, :] = total
                acc_ratio[d, at : at + 8, :] = ratio

    multiply(0)
    for b in range(BANDS):
        if b + 1 < BANDS:
            multiply(b + 1)
        reduce(b)

    flip = jnp.where(
        lax.broadcasted_iota(jnp.int32, (DBLK, ZR), 0)
        + lax.broadcasted_iota(jnp.int32, (DBLK, ZR), 1)
        == DBLK,
        1.0,
        0.0,
    )
    first, last, rated = retina[j, 0], retina[j, 1], qblock[0, j]
    score = jnp.zeros((1, lines), jnp.float32)
    for d in range(NDB):
        ratio, power = acc_ratio[d], acc_power[d]
        dec = 1.0 - ratio * (2.0 / (BANDS * (repeats - 1)))
        struct = jnp.log(power * (1.0 / (BANDS * repeats)) + 0.05)
        if d % 2:
            dec = jnp.dot(flip, dec, precision=lax.Precision.HIGHEST)
            struct = jnp.dot(flip, struct, precision=lax.Precision.HIGHEST)
        else:
            dec, struct = dec[:DBLK], struct[:DBLK]
        inside = (first <= d) & (d <= last)
        dec_out[d * DBLK : (d + 1) * DBLK, :] = jnp.where(inside, dec, 0.0)
        str_out[d * DBLK : (d + 1) * DBLK, :] = jnp.where(inside, struct, 0.0)
        score = score + jnp.where(rated == d, jnp.sum(struct, axis=0, keepdims=True), 0.0)
    mean = jnp.sum(score, axis=1, keepdims=True) * (1.0 / (DBLK * lines)) + bias[0, j]
    score_out[pl.ds(j, 1), :] = jnp.broadcast_to(mean, (1, score_out.shape[1]))


def compute(spectra, block_scales, retina, qblock, bias):
    _, repeats, lines, samples = spectra.shape
    kb = block_scales.shape[3]
    tiles = lines // ABLK
    inner = samples // CLASSES
    cols = repeats * ABLK
    smem = pl.BlockSpec(memory_space=pltpu.SMEM)
    score_rows = -(-tiles // 8) * 8
    return pl.pallas_call(
        compute_kernel,
        grid=(tiles,),
        out_shape=(
            jax.ShapeDtypeStruct((DEPTH, lines), jnp.float32),
            jax.ShapeDtypeStruct((DEPTH, lines), jnp.float32),
            jax.ShapeDtypeStruct((score_rows, 128), jnp.float32),
        ),
        in_specs=[
            smem, smem, smem,
            pl.BlockSpec((1, repeats, ABLK, samples), lambda j: (0, 0, j, 0)),
            pl.BlockSpec((1, repeats, ABLK, kb), lambda j: (0, 0, j, 0)),
        ],
        out_specs=(
            pl.BlockSpec((DEPTH, ABLK), lambda j: (0, j)),
            pl.BlockSpec((DEPTH, ABLK), lambda j: (0, j)),
            pl.BlockSpec((score_rows, 128), lambda j: (0, 0)),
        ),
        scratch_shapes=[
            pltpu.VMEM((CLASSES, BANDS * 2 * ZR, inner), jnp.bfloat16),
            pltpu.VMEM((256, 256), jnp.bfloat16),
            pltpu.VMEM((CLASSES, inner, cols), jnp.bfloat16),
            pltpu.VMEM((CLASSES, 2 * ZR, cols), jnp.float32),
            pltpu.VMEM((CLASSES, 2 * ZR, cols), jnp.float32),
            pltpu.VMEM((NDB, ZR, ABLK), jnp.float32),
            pltpu.VMEM((NDB, ZR, ABLK), jnp.float32),
        ],
        compiler_params=pltpu.CompilerParams(vmem_limit_bytes=48 * 1024 * 1024),
    )(retina, qblock, bias, spectra, block_scales)


def join_kernel(
    n, dec, struct, score, ang_out, str_out, spread_out,
    rdec, rstr, rscore, redge, ssem, rsem, lsem, esem,
):
    rows = dec.shape[0] // n
    lines = dec.shape[1]
    tiles = lines // ABLK
    me, t = lax.axis_index("vol"), lax.axis_index("tile")
    other = 1 - t
    barrier = pltpu.get_barrier_semaphore()
    for d in range(1, n):
        pl.semaphore_signal(barrier, inc=1, device_id={"vol": (me + d) % n}, device_id_type=MESH)
    pl.semaphore_signal(barrier, inc=1, device_id={"tile": other}, device_id_type=MESH)
    pl.semaphore_wait(barrier, n)

    def pieces(target):
        at = pl.ds(pl.multiple_of(target * rows, 8), rows)
        return (
            (score, rscore.at[me]),
            (dec.at[at, :], rdec.at[me]),
            (struct.at[at, :], rstr.at[me]),
        )

    copies = {}
    for kind in range(3):
        for d in range(1, n):
            target = (me + d) % n
            src, dst = pieces(target)[kind]
            copies[kind, d] = pltpu.make_async_remote_copy(
                src_ref=src, dst_ref=dst, send_sem=ssem.at[kind, d], recv_sem=rsem.at[kind, d],
                device_id={"vol": target}, device_id_type=MESH,
            )
            copies[kind, d].start()
    local = []
    for kind in range(3):
        src, dst = pieces(me)[kind]
        local.append(pltpu.make_async_copy(src, dst, lsem.at[kind]))
        local[-1].start()
    for c in local:
        c.wait()
    for d in range(1, n):
        copies[0, d].wait_recv()
        copies[1, d].wait_recv()
    column = pl.multiple_of((1 - t) * (lines - ABLK), ABLK)
    edge = pltpu.make_async_remote_copy(
        src_ref=rdec.at[:, :, pl.ds(column, ABLK)], dst_ref=redge,
        send_sem=esem.at[0], recv_sem=esem.at[1],
        device_id={"tile": other}, device_id_type=MESH,
    )
    edge.start()
    scores = rscore[...]
    top = jnp.max(scores, axis=0, keepdims=True)
    grown = jnp.exp(scores - top)
    weights = grown / jnp.sum(grown, axis=0, keepdims=True)
    for d in range(1, n):
        copies[2, d].wait_recv()
    edge.wait_recv()
    lane = lax.broadcasted_iota(jnp.int32, (rows, ABLK), 1)
    near = (lane >= t * (ABLK - 2)) & (lane < 2 + t * ABLK)
    width = lines + ABLK
    ang = [jnp.zeros((rows, ABLK), jnp.float32)] * tiles
    square = list(ang)
    joined = list(ang)
    for v in range(n):
        wide = jnp.concatenate([rdec[v], jnp.where(near, redge[v], 0.0)], axis=1)
        smooth = (
            (pltpu.roll(wide, 2, 1) + pltpu.roll(wide, width - 2, 1)) * (1.0 / 9.0)
            + (pltpu.roll(wide, 1, 1) + pltpu.roll(wide, width - 1, 1)) * (2.0 / 9.0)
            + wide * (3.0 / 9.0)
        )
        for j in range(tiles):
            w = weights[v, j : j + 1, :]
            s = smooth[:, j * ABLK : (j + 1) * ABLK]
            ws = w * s
            ang[j] = ang[j] + ws
            square[j] = square[j] + ws * s
            joined[j] = joined[j] + w * rstr[v, :, j * ABLK : (j + 1) * ABLK]
    for j in range(tiles):
        at = slice(j * ABLK, (j + 1) * ABLK)
        ang_out[:, at] = ang[j]
        str_out[:, at] = joined[j]
        spread_out[:, at] = jnp.sqrt(square[j] - ang[j] * ang[j] + 0.01)
    for c in copies.values():
        c.wait_send()
    edge.wait_send()


def join(n, dec, struct, score):
    depth, lines = dec.shape
    rows = depth // n
    vmem = pl.BlockSpec(memory_space=pltpu.VMEM)
    out = jax.ShapeDtypeStruct((rows, lines), jnp.float32)
    return pl.pallas_call(
        functools.partial(join_kernel, n),
        out_shape=(out, out, out),
        in_specs=[vmem] * 3,
        out_specs=(vmem,) * 3,
        scratch_shapes=[
            pltpu.VMEM((n, rows, lines), jnp.float32),
            pltpu.VMEM((n, rows, lines), jnp.float32),
            pltpu.VMEM((n,) + score.shape, jnp.float32),
            pltpu.VMEM((n, rows, ABLK), jnp.float32),
            pltpu.SemaphoreType.DMA((3, n)),
            pltpu.SemaphoreType.DMA((3, n)),
            pltpu.SemaphoreType.DMA((3,)),
            pltpu.SemaphoreType.DMA((2,)),
        ],
        compiler_params=pltpu.CompilerParams(collective_id=0, has_side_effects=True),
    )(dec, struct, score)


def solution(mesh):
    n = mesh.shape["vol"]
    assert mesh.shape["tile"] == 2

    def on_device(spectra, block_scales, retina_blocks, quality_block, quality_bias):
        dec, struct, score = compute(
            spectra, block_scales, retina_blocks, quality_block, quality_bias
        )
        return join(n, dec, struct, score)

    return jax.shard_map(
        on_device,
        mesh=mesh,
        in_specs=(
            P(("study", "vol"), None, "tile", None),
            P(("study", "vol"), None, "tile", None),
            P(("study", "tile"), None),
            P(("study", "vol"), "tile"),
            P(("study", "vol"), "tile"),
        ),
        out_specs=(
            P(("study", "vol"), "tile"),
            P(("study", "vol"), "tile"),
            P(("study", "vol"), "tile"),
        ),
        check_vma=False,
    )
```

time: 235 us -> 77.5 us (0.33); the launches traced: 230 us -> 77.2 us
  waiting for transfers between devices: 74 us -> 0 us
  other arithmetic: 72.3 us -> 0 us
  Pallas kernels: 0 us -> 66.3 us
  matrix products: 36.1 us -> 0 us
  between operations: 14.3 us -> 0.68 us
  blocking collectives: 10.5 us -> 0 us
  local copies, waits for them, and re-layouts: 18.8 us -> 10.2 us
  starting transfers between devices: 4.37 us -> 0 us
    reduce_scatter x1 -> x0, waiting for transfers between devices: 74 us -> none  [on_device(): lax.psum_scatter(stacked, 'vol', scatter_dimension=1, tiled=True)]
    pallas_call x0 -> x2, Pallas kernels: none -> 66.3 us  [the longest x1 43 us: join(): pl.pallas_call(functools.partial(join_kernel, n), out_shape=(out, out, ou...]
    dot_general x4 -> x0, matrix products: 36.1 us -> none  [band_maps(): jnp.einsum('kcd,rak->cdra', tables[band_index], scaled, preferred_element...]
    reduce_sum x12 -> x0, other arithmetic: 19.2 us -> none  [the longest x4 16.5 us: band_maps(): decorrelation = decorrelation + jnp.sum(1.0 - pair_ratio, axis=1)]
    neg x1 -> x0, other arithmetic: 17.7 us -> none  [window_tables(): kernel = jnp.stack([jnp.cos(phase_angle), -jnp.sin(phase_angle)], axis=1)]
    sqrt x5 -> x0, other arithmetic: 14.1 us -> none  [the longest x4 12.5 us: band_maps(): amplitude = jnp.sqrt(band_power + 0.05)]
    convert_element_type x3 -> x0, other arithmetic: 12.2 us -> none  [the longest x1 6.29 us: window_tables(): return (window[:, :, None, None] * kernel[None]).astype(jnp.bfloat16)]
    all_gather x1 -> x0, blocking collectives: 10.5 us -> none  [on_device(): scores = lax.all_gather(volume_score[None, :], 'vol', axis=0, tiled=True)]
  transfers between devices with their start and end apart: 3 -> 0, of which waited for: 1 -> 0; matrix products, arithmetic and copies ran while one was open for 2% -> 0% of each run, Pallas kernels for 0% -> 0%
where the time goes in v1:
time: 77.5 us; the launch traced here: 77.2 us
  Pallas kernels  66.3 us (86%)
  local copies, waits for them, and re-layouts  10.2 us (13%)
    pallas_call x1, Pallas kernels, join(): pl.pallas_call(functools.partial(join_kernel, n), out_shape=(out, out, ou...  43 us
    pallas_call x1, Pallas kernels, compute(): pl.pallas_call(compute_kernel, grid=(tiles,), out_shape=(jax.ShapeDtypeSt...  23.3 us
    unnamed x15, local copies, waits for them, and re-layouts  10.2 us

profile of v1, /device:TPU:13, one launch (start us, length us, event | category | flops | bytes accessed | tf_op | source)
XLA Modules:
  0.0 77.2 jit_solution(5029325090497872703)
XLA Ops:
  0.6 0.8 copy.8.retina
  1.4 1.2 %copy.9.scales = f32[1,4,384,16]{3,2,1,0:T(8,128)S(1)} copy(f32[1,4,384,16]{2,3,1,0:T(8,128)} %param.6) | data formatting | bytes 196608 | tf_op args[1]
  2.6 0.0 copy-start.3
  2.6 0.6 copy-done.3
  3.2 0.0 copy-start.4
  3.2 0.7 copy-done.4
  3.9 23.3 %shard_map.76 = (f32[512,384]{1,0:T(8,128)S(1)}, f32[512,384]{1,0:T(8,128)S(1)}, f32[8,128]{1,0:T(8,128)S(1)}) custom-call(s32[3,2]{1,0:T(4,128)S(1)} %copy.8.retina, s32[1,3]{1,0:T(1,128)S(1)} %copy-done.3, f32[1,3]{1,0:T(1,128)S(1)} %copy-done.4, bf16[1,4,384,2048]{3,2,1,0:T(8,128)(2,1)} %spec.1, f32[1,4,384,16]{3,2,1,0:T(8,128)S(1)} %copy.9.scales), custom_call_target="tpu_custom_call" | custom-call | tf_op jit(solution)/shard_map/pallas_call | solution.py:181
  27.2 0.0 copy-start
  27.2 0.9 %copy-done = f32[512,384]{1,0:T(8,128)} copy-done((f32[512,384]{1,0:T(8,128)}, f32[512,384]{1,0:T(8,128)S(1)}, u32[]{:S(2)}) %copy-start) | copy-done | bytes 786456
  28.1 0.0 copy-start.1
  28.1 0.9 %copy-done.1 = f32[512,384]{1,0:T(8,128)} copy-done((f32[512,384]{1,0:T(8,128)}, f32[512,384]{1,0:T(8,128)S(1)}, u32[]{:S(2)}) %copy-start.1) | copy-done | bytes 786456
  29.0 0.0 copy-start.2
  29.0 0.6 copy-done.2
  29.5 43.0 %shard_map.77 = (f32[64,384]{1,0:T(8,128)}, f32[64,384]{1,0:T(8,128)}, f32[64,384]{1,0:T(8,128)}) custom-call(f32[512,384]{1,0:T(8,128)} %copy-done, f32[512,384]{1,0:T(8,128)} %copy-done.1, f32[8,128]{1,0:T(8,128)} %copy-done.2), custom_call_target="tpu_custom_call" | custom-call | tf_op jit(solution)/shard_map/pallas_call | solution.py:304
  72.6 1.5 %copy.13 = f32[64,384]{1,0:T(8,128)} copy(f32[64,384]{1,0:T(8,128)} %get-tuple-element.12) | data formatting | bytes 196608
  74.1 1.5 %copy.14 = f32[64,384]{1,0:T(8,128)} copy(f32[64,384]{1,0:T(8,128)} %get-tuple-element.13) | data formatting | bytes 196608
  75.7 1.5 %copy.15 = f32[64,384]{1,0:T(8,128)} copy(f32[64,384]{1,0:T(8,128)} %get-tuple-element.14) | data formatting | bytes 196608
Async XLA Ops:
  2.6 0.7 copy-start.3
  3.2 0.7 copy-start.4
  27.2 0.9 %copy-start = (f32[512,384]{1,0:T(8,128)}, f32[512,384]{1,0:T(8,128)S(1)}, u32[]{:S(2)}) copy-start(f32[512,384]{1,0:T(8,128)S(1)} %get-tuple-element.6.dec) | copy-start | bytes 2359300
  28.1 0.9 %copy-start.1 = (f32[512,384]{1,0:T(8,128)}, f32[512,384]{1,0:T(8,128)S(1)}, u32[]{:S(2)}) copy-start(f32[512,384]{1,0:T(8,128)S(1)} %get-tuple-element.7.struct) | copy-start | bytes 2359300
  29.0 0.6 copy-start.2

commit v2 on v1

v2 whole, which is shorter than its diff:
```python
import functools
import math

import jax
import jax.numpy as jnp
from jax import lax
from jax.experimental import pallas as pl
from jax.experimental.pallas import tpu as pltpu
from jax.sharding import PartitionSpec as P

DEPTH = 512
BANDS = 4
DBLK = 128
ABLK = 128
SB = 128
NDB = 4
CLASSES = 8
MESH = pl.DeviceIdType.MESH
ZR = 136


def build_tables(table, perm, samples):
    inner = samples // CLASSES
    z = lax.broadcasted_iota(jnp.int32, (ZR, inner), 0)
    k1 = lax.broadcasted_iota(jnp.int32, (ZR, inner), 1)
    unit = 2.0 * math.pi / samples
    base = ((CLASSES * k1 * z) % samples).astype(jnp.float32) * unit
    step = z.astype(jnp.float32) * unit
    re, im = jnp.cos(base), -jnp.sin(base)
    sre, sim = jnp.cos(step), -jnp.sin(step)
    kk = (
        lax.broadcasted_iota(jnp.int32, (CLASSES, inner), 1) * CLASSES
        + lax.broadcasted_iota(jnp.int32, (CLASSES, inner), 0)
    ).astype(jnp.float32)
    windows = []
    for b in range(BANDS):
        distance = kk - (b + 0.5) * (samples / BANDS)
        offset = distance / (samples / 8.0)
        g = jnp.where(jnp.abs(distance) <= samples / 2.0, jnp.exp(-0.5 * offset * offset), 0.0)
        windows.append(g / jnp.sqrt(jnp.sum(g * g, keepdims=True)))
    for k0 in range(CLASSES):
        if k0:
            re, im = re * sre - im * sim, re * sim + im * sre
        both = jnp.concatenate([re, im], axis=0)
        for b in range(BANDS):
            row = windows[b][k0 : k0 + 1, :]
            table[k0, b * 2 * ZR : (b + 1) * 2 * ZR, :] = (both * row).astype(jnp.bfloat16)
    size = perm.shape[0]
    part = size // CLASSES
    row = lax.broadcasted_iota(jnp.int32, (size, size), 0)
    col = lax.broadcasted_iota(jnp.int32, (size, size), 1)
    perm[...] = jnp.where(col == (row % part) * CLASSES + row // part, 1.0, 0.0).astype(jnp.bfloat16)


def combine(get):
    rr, ii = [get(k, 0) for k in range(8)], [get(k, 1) for k in range(8)]
    sr = [rr[j] + rr[j + 4] for j in range(4)]
    si = [ii[j] + ii[j + 4] for j in range(4)]
    dr = [rr[j] - rr[j + 4] for j in range(4)]
    di = [ii[j] - ii[j + 4] for j in range(4)]
    half = math.sqrt(0.5)
    re0, im0 = (sr[0] + sr[2]) + (sr[1] + sr[3]), (si[0] + si[2]) + (si[1] + si[3])
    re3, im3 = (sr[0] - sr[2]) - (si[1] - si[3]), (si[0] - si[2]) + (sr[1] - sr[3])
    p, q = (dr[1] - dr[3]) * half, (di[1] + di[3]) * half
    r, t = (di[1] - di[3]) * half, (dr[1] + dr[3]) * half
    re2, im2 = (dr[0] + di[2]) + (p + q), (di[0] - dr[2]) + (r - t)
    re1, im1 = (dr[0] - di[2]) + (p - q), (di[0] + dr[2]) + (r + t)
    fields = ((re0, im0), (re1, im1), (re2, im2), (re3, im3))
    return [re * re + (im * im + 0.05) for re, im in fields]


def fused_kernel(
    retina, qblock, bias, spec, scales, joined_out,
    table, perm, data, ga, gb, acc_ratio, acc_power,
    sent, got, redge, ssem, rsem, lsem, esem,
):
    j = pl.program_id(0)
    repeats, lines, samples = spec.shape[1:]
    chunk = perm.shape[0]
    tiles, n = sent.shape[:2]
    rows = redge.shape[1]
    me, t = lax.axis_index("vol"), lax.axis_index("tile")
    other = 1 - t
    part = chunk // CLASSES
    cols = repeats * lines

    @pl.when(j == 0)
    def _():
        barrier = pltpu.get_barrier_semaphore()
        for d in range(1, n):
            pl.semaphore_signal(
                barrier, inc=1, device_id={"vol": (me + d) % n}, device_id_type=MESH
            )
        pl.semaphore_signal(barrier, inc=1, device_id={"tile": other}, device_id_type=MESH)
        build_tables(table, perm, samples)

    scale_t = jnp.concatenate([scales[0, r] for r in range(repeats)], axis=1)
    for q in range(samples // chunk):
        block = spec[0, :, :, q * chunk : (q + 1) * chunk].reshape(cols, chunk)
        moved = lax.dot_general(
            perm[...], block, (((1,), (1,)), ((), ())), preferred_element_type=jnp.float32
        )
        per = chunk // SB
        factor = jnp.concatenate(
            [
                jnp.broadcast_to(scale_t[q * per + h : q * per + h + 1, :], (part // per, cols))
                for h in range(per)
            ],
            axis=0,
        )
        for k0 in range(CLASSES):
            data[k0, q * part : (q + 1) * part, :] = (
                moved[k0 * part : (k0 + 1) * part] * factor
            ).astype(jnp.bfloat16)

    buffers = (ga, gb)

    def multiply(b):
        for k0 in range(CLASSES):
            buffers[b % 2][k0] = jnp.dot(
                table[k0, b * 2 * ZR : (b + 1) * 2 * ZR, :],
                data[k0],
                preferred_element_type=jnp.float32,
            )

    def reduce(b):
        g = buffers[b % 2]

        for i in range(ZR // 8):
            at = i * 8
            powers = []
            for r in range(repeats):
                def get(k, c):
                    return g[k, c * ZR + at : c * ZR + at + 8, r * lines : (r + 1) * lines]

                powers.append(combine(get))
            for d in range(NDB):
                total = powers[0][d]
                ratio = None
                for r in range(repeats - 1):
                    first, second = powers[r][d], powers[r + 1][d]
                    total = total + second
                    prod, both = first * second, first + second
                    term = prod * lax.rsqrt(prod * (both * both))
                    ratio = term if ratio is None else ratio + term
                if b:
                    total = total + acc_power[d, at : at + 8, :]
                    ratio = ratio + acc_ratio[d, at : at + 8, :]
                acc_power[d, at : at + 8, :] = total
                acc_ratio[d, at : at + 8, :] = ratio

    multiply(0)
    for b in range(BANDS):
        if b + 1 < BANDS:
            multiply(b + 1)
        reduce(b)

    flip = jnp.where(
        lax.broadcasted_iota(jnp.int32, (DBLK, ZR), 0)
        + lax.broadcasted_iota(jnp.int32, (DBLK, ZR), 1)
        == DBLK,
        1.0,
        0.0,
    )
    first, last, rated = retina[0, j], retina[1, j], qblock[0, j]
    score = jnp.zeros((1, lines), jnp.float32)
    for d in range(NDB):
        ratio, power = acc_ratio[d], acc_power[d]
        dec = 1.0 - ratio * (2.0 / (BANDS * (repeats - 1)))
        struct = jnp.log(power * (1.0 / (BANDS * repeats)) + 0.05)
        if d % 2:
            dec = jnp.dot(flip, dec, precision=lax.Precision.HIGHEST)
            struct = jnp.dot(flip, struct, precision=lax.Precision.HIGHEST)
        else:
            dec, struct = dec[:DBLK], struct[:DBLK]
        inside = (first <= d) & (d <= last)
        score = score + jnp.where(rated == d, jnp.sum(struct, axis=0, keepdims=True), 0.0)
        dec, struct = jnp.where(inside, dec, 0.0), jnp.where(inside, struct, 0.0)
        per = DBLK // rows
        for s in range(per):
            sent[j, d * per + s, :rows, :] = dec[s * rows : (s + 1) * rows]
            sent[j, d * per + s, rows : 2 * rows, :] = struct[s * rows : (s + 1) * rows]
    mean = jnp.sum(score, axis=1, keepdims=True) * (1.0 / (DBLK * lines)) + bias[0, j]
    for u in range(n):
        sent[j, u, 2 * rows :, :] = jnp.broadcast_to(mean, (8, lines))

    def remote(step, d):
        target = (me + d) % n
        return pltpu.make_async_remote_copy(
            src_ref=sent.at[step, target], dst_ref=got.at[step, me],
            send_sem=ssem.at[step, d], recv_sem=rsem.at[step, d],
            device_id={"vol": target}, device_id_type=MESH,
        )

    def local(step):
        return pltpu.make_async_copy(sent.at[step, me], got.at[step, me], lsem.at[step])

    @pl.when(j == 0)
    def _():
        pl.semaphore_wait(pltpu.get_barrier_semaphore(), n)

    for d in range(1, n):
        remote(j, d).start()
    local(j).start()

    @pl.when(j == tiles - 1)
    def _():
        for step in range(tiles):
            local(step).wait()
            for d in range(1, n):
                remote(step, d).wait_recv()
        edge = pltpu.make_async_remote_copy(
            src_ref=got.at[other * (tiles - 1), :, pl.ds(0, rows), :], dst_ref=redge,
            send_sem=esem.at[0], recv_sem=esem.at[1],
            device_id={"tile": other}, device_id_type=MESH,
        )
        edge.start()
        weights = []
        for step in range(tiles):
            scores = [got[step, v, 2 * rows : 2 * rows + 1, :] for v in range(n)]
            top = functools.reduce(jnp.maximum, scores)
            grown = [jnp.exp(x - top) for x in scores]
            total = functools.reduce(jnp.add, grown)
            weights.append([x / total for x in grown])
        for step in range(tiles):
            at = slice(step * lines, (step + 1) * lines)
            total = jnp.zeros((rows, lines), jnp.float32)
            for v in range(n):
                total = total + weights[step][v] * got[step, v, rows : 2 * rows, :]
            joined_out[2, :, at] = total
        lane = lax.broadcasted_iota(jnp.int32, (rows, lines), 1)
        near = (lane >= t * (lines - 2)) & (lane < 2 + t * lines)
        width = (tiles + 1) * lines
        ang = [jnp.zeros((rows, lines), jnp.float32)] * tiles
        square = list(ang)
        edge.wait_recv()
        for v in range(n):
            wide = jnp.concatenate(
                [got[step, v, :rows, :] for step in range(tiles)]
                + [jnp.where(near, redge[v], 0.0)],
                axis=1,
            )
            smooth = (
                (pltpu.roll(wide, 2, 1) + pltpu.roll(wide, width - 2, 1)) * (1.0 / 9.0)
                + (pltpu.roll(wide, 1, 1) + pltpu.roll(wide, width - 1, 1)) * (2.0 / 9.0)
                + wide * (3.0 / 9.0)
            )
            for step in range(tiles):
                w = weights[step][v]
                s = smooth[:, step * lines : (step + 1) * lines]
                ws = w * s
                ang[step] = ang[step] + ws
                square[step] = square[step] + ws * s
        for step in range(tiles):
            at = slice(step * lines, (step + 1) * lines)
            joined_out[0, :, at] = ang[step]
            joined_out[1, :, at] = square[step]
        for step in range(tiles):
            for d in range(1, n):
                remote(step, d).wait_send()
        edge.wait_send()


def fused(n, spectra, block_scales, retina, qblock, bias):
    _, repeats, lines, samples = spectra.shape
    kb = block_scales.shape[3]
    tiles = lines // ABLK
    inner = samples // CLASSES
    cols = repeats * ABLK
    rows = DEPTH // n
    smem = pl.BlockSpec(memory_space=pltpu.SMEM)
    return pl.pallas_call(
        fused_kernel,
        grid=(tiles,),
        out_shape=jax.ShapeDtypeStruct((3, rows, lines), jnp.float32),
        in_specs=[
            smem, smem, smem,
            pl.BlockSpec((1, repeats, ABLK, samples), lambda j: (0, 0, j, 0)),
            pl.BlockSpec((1, repeats, kb, ABLK), lambda j: (0, 0, 0, j)),
        ],
        out_specs=pl.BlockSpec((3, rows, lines), lambda j: (0, 0, 0)),
        scratch_shapes=[
            pltpu.VMEM((CLASSES, BANDS * 2 * ZR, inner), jnp.bfloat16),
            pltpu.VMEM((256, 256), jnp.bfloat16),
            pltpu.VMEM((CLASSES, inner, cols), jnp.bfloat16),
            pltpu.VMEM((CLASSES, 2 * ZR, cols), jnp.float32),
            pltpu.VMEM((CLASSES, 2 * ZR, cols), jnp.float32),
            pltpu.VMEM((NDB, ZR, ABLK), jnp.float32),
            pltpu.VMEM((NDB, ZR, ABLK), jnp.float32),
            pltpu.VMEM((tiles, n, 2 * rows + 8, ABLK), jnp.float32),
            pltpu.VMEM((tiles, n, 2 * rows + 8, ABLK), jnp.float32),
            pltpu.VMEM((n, rows, ABLK), jnp.float32),
            pltpu.SemaphoreType.DMA((tiles, n)),
            pltpu.SemaphoreType.DMA((tiles, n)),
            pltpu.SemaphoreType.DMA((tiles,)),
            pltpu.SemaphoreType.DMA((2,)),
        ],
        compiler_params=pltpu.CompilerParams(
            vmem_limit_bytes=48 * 1024 * 1024, collective_id=0, has_side_effects=True
        ),
    )(retina.T, qblock, bias, spectra, block_scales.transpose(0, 1, 3, 2))


def finish_kernel(joined, ang_out, str_out, spread_out):
    ang = joined[0]
    ang_out[...] = ang
    str_out[...] = joined[2]
    spread_out[...] = jnp.sqrt(joined[1] - ang * ang + 0.01)


def finish(joined):
    out = jax.ShapeDtypeStruct(joined.shape[1:], jnp.float32)
    return pl.pallas_call(finish_kernel, out_shape=(out, out, out))(joined)


def solution(mesh):
    n = mesh.shape["vol"]
    assert mesh.shape["tile"] == 2

    def on_device(spectra, block_scales, retina_blocks, quality_block, quality_bias):
        return finish(
            fused(n, spectra, block_scales, retina_blocks, quality_block, quality_bias)
        )

    return jax.shard_map(
        on_device,
        mesh=mesh,
        in_specs=(
            P(("study", "vol"), None, "tile", None),
            P(("study", "vol"), None, "tile", None),
            P(("study", "tile"), None),
            P(("study", "vol"), "tile"),
            P(("study", "vol"), "tile"),
        ),
        out_specs=(
            P(("study", "vol"), "tile"),
            P(("study", "vol"), "tile"),
            P(("study", "vol"), "tile"),
        ),
        check_vma=False,
    )
```

time: 77.5 us -> 58.1 us (0.75)
  Pallas kernels: 66.3 us -> 53.5 us
  local copies, waits for them, and re-layouts: 10.2 us -> 3.58 us
    pallas_call x2, Pallas kernels: 66.3 us -> 53.5 us  [the longest x1 51.8 us: fused(): pl.pallas_call(fused_kernel, grid=(tiles,), out_shape=jax.ShapeDtypeStruc...]
    unnamed x15 -> x10, local copies, waits for them, and re-layouts: 10.2 us -> 3.58 us
where the time goes in v2:
time: 58.1 us; the launch traced here: 57.7 us
  Pallas kernels  53.5 us (92%)
  local copies, waits for them, and re-layouts  3.58 us (6%)
  between operations  0.66 us (1%)
    pallas_call x1, Pallas kernels, fused(): pl.pallas_call(fused_kernel, grid=(tiles,), out_shape=jax.ShapeDtypeStruc...  51.8 us
    unnamed x10, local copies, waits for them, and re-layouts  3.58 us
    pallas_call x1, Pallas kernels, finish(): return pl.pallas_call(finish_kernel, out_shape=(out, out, out))(joined)  1.67 us

profile of v2, /device:TPU:13, one launch (start us, length us, event | category | flops | bytes accessed | tf_op | source)
XLA Modules:
  0.0 57.7 jit_solution(16806800165997849119)
XLA Ops:
  0.6 0.0 copy-start.1
  0.6 0.9 %copy-done.1 = f32[1,4,384,16]{2,3,1,0:T(8,128)S(1)} copy-done((f32[1,4,384,16]{2,3,1,0:T(8,128)S(1)}, f32[1,4,384,16]{2,3,1,0:T(8,128)}, u32[]{:S(2)}) %copy-start.1) | copy-done | bytes 98328
  1.5 0.0 copy-start.2
  1.5 0.7 %copy-done.2 = s32[3,2]{0,1:T(2,128)S(1)} copy-done((s32[3,2]{0,1:T(2,128)S(1)}, s32[3,2]{0,1:T(2,128)}, u32[]{:S(2)}) %copy-start.2) | copy-done | bytes 48
  2.2 0.0 copy-start.3
  2.2 0.7 %copy-done.3 = s32[1,3]{1,0:T(1,128)S(1)} copy-done((s32[1,3]{1,0:T(1,128)S(1)}, s32[1,3]{1,0:T(1,128)}, u32[]{:S(2)}) %copy-start.3) | copy-done | bytes 36
  2.9 0.0 copy-start.4
  2.9 0.7 %copy-done.4 = f32[1,3]{1,0:T(1,128)S(1)} copy-done((f32[1,3]{1,0:T(1,128)S(1)}, f32[1,3]{1,0:T(1,128)}, u32[]{:S(2)}) %copy-start.4) | copy-done | bytes 36
  3.5 51.8 %shard_map.76.joined = f32[3,64,384]{2,1,0:T(8,128)S(1)} custom-call(s32[2,3]{1,0:T(2,128)S(1)} %bitcast.3, s32[1,3]{1,0:T(1,128)S(1)} %copy-done.3, f32[1,3]{1,0:T(1,128)S(1)} %copy-done.4, bf16[1,4,384,2048]{3,2,1,0:T(8,128)(2,1)} %spec.1, f32[1,4,16,384]{3,2,1,0:T(8,128)S(1)} %bitcast.2), custom_call_target="tpu_custom_call" | custom-call | tf_op jit(solution)/shard_map/pallas_call | solution.py:272
  55.3 0.0 copy-start
  55.3 0.7 %copy-done = f32[3,64,384]{2,1,0:T(8,128)} copy-done((f32[3,64,384]{2,1,0:T(8,128)}, f32[3,64,384]{2,1,0:T(8,128)S(1)}, u32[]{:S(2)}) %copy-start) | copy-done | bytes 294936
  56.0 1.7 %shard_map.77 = (f32[64,384]{1,0:T(8,128)}, f32[64,384]{1,0:T(8,128)}, f32[64,384]{1,0:T(8,128)}) custom-call(f32[3,64,384]{2,1,0:T(8,128)} %copy-done), custom_call_target="tpu_custom_call" | custom-call | tf_op jit(solution)/shard_map/pallas_call | solution.py:313
Async XLA Ops:
  0.6 0.9 %copy-start.1 = (f32[1,4,384,16]{2,3,1,0:T(8,128)S(1)}, f32[1,4,384,16]{2,3,1,0:T(8,128)}, u32[]{:S(2)}) copy-start(f32[1,4,384,16]{2,3,1,0:T(8,128)} %param.6) | copy-start | bytes 294916
  1.5 0.7 %copy-start.2 = (s32[3,2]{0,1:T(2,128)S(1)}, s32[3,2]{0,1:T(2,128)}, u32[]{:S(2)}) copy-start(s32[3,2]{0,1:T(2,128)} %param.7) | copy-start | bytes 76
  2.2 0.7 %copy-start.3 = (s32[1,3]{1,0:T(1,128)S(1)}, s32[1,3]{1,0:T(1,128)}, u32[]{:S(2)}) copy-start(s32[1,3]{1,0:T(1,128)} %qblock.1) | copy-start | bytes 40
  2.9 0.7 %copy-start.4 = (f32[1,3]{1,0:T(1,128)S(1)}, f32[1,3]{1,0:T(1,128)}, u32[]{:S(2)}) copy-start(f32[1,3]{1,0:T(1,128)} %bias.1) | copy-start | bytes 40
  55.3 0.7 %copy-start = (f32[3,64,384]{2,1,0:T(8,128)}, f32[3,64,384]{2,1,0:T(8,128)S(1)}, u32[]{:S(2)}) copy-start(f32[3,64,384]{2,1,0:T(8,128)S(1)} %shard_map.76.joined) | copy-start | bytes 884740

commit v3 on v2

--- a/solution.py
+++ b/solution.py
@@ -296,7 +296,7 @@
             pltpu.SemaphoreType.DMA((2,)),
         ],
         compiler_params=pltpu.CompilerParams(
-            vmem_limit_bytes=48 * 1024 * 1024, collective_id=0, has_side_effects=True
+            vmem_limit_bytes=67043328, collective_id=0, has_side_effects=True
         ),
     )(retina.T, qblock, bias, spectra, block_scales.transpose(0, 1, 3, 2))
 

time: 58.1 us -> 55.2 us (0.950)
  local copies, waits for them, and re-layouts: 3.58 us -> 0 us
  Pallas kernels: 53.5 us -> 54.2 us
    unnamed x10 -> x0, local copies, waits for them, and re-layouts: 3.58 us -> none
    pallas_call x1, Pallas kernels: 51.8 us -> 52.5 us  [fused(): pl.pallas_call(fused_kernel, grid=(tiles,), out_shape=jax.ShapeDtypeStruc...]
where the time goes in v3:
time: 55.2 us; the launch traced here: 54.8 us
  Pallas kernels  54.2 us (98%)
  between operations  0.64 us (1%)
    pallas_call x1, Pallas kernels, fused(): pl.pallas_call(fused_kernel, grid=(tiles,), out_shape=jax.ShapeDtypeStruc...  52.5 us
    pallas_call x1, Pallas kernels, finish(): return pl.pallas_call(finish_kernel, out_shape=(out, out, out))(joined)  1.67 us

profile of v3, /device:TPU:13, one launch (start us, length us, event | category | flops | bytes accessed | tf_op | source)
XLA Modules:
  0.0 54.8 jit_solution(5108254062436405394)
XLA Ops:
  0.6 52.5 %shard_map.76.joined = f32[3,64,384]{2,1,0:T(8,128)} custom-call(s32[2,3]{1,0:T(2,128)} %bitcast.3, s32[1,3]{1,0:T(1,128)} %qblock.1, f32[1,3]{1,0:T(1,128)} %bias.1, bf16[1,4,384,2048]{3,2,1,0:T(8,128)(2,1)} %spec.1, f32[1,4,16,384]{3,2,1,0:T(8,128)} %bitcast.2), custom_call_target="tpu_custom_call" | custom-call | tf_op jit(solution)/shard_map/pallas_call | solution.py:272
  53.1 1.7 %shard_map.77 = (f32[64,384]{1,0:T(8,128)}, f32[64,384]{1,0:T(8,128)}, f32[64,384]{1,0:T(8,128)}) custom-call(f32[3,64,384]{2,1,0:T(8,128)} %shard_map.76.joined), custom_call_target="tpu_custom_call" | custom-call | tf_op jit(solution)/shard_map/pallas_call | solution.py:313

commit v4 on v3

--- a/solution.py
+++ b/solution.py
@@ -72,15 +72,19 @@
 def fused_kernel(
     retina, qblock, bias, spec, scales, joined_out,
     table, perm, data, ga, gb, acc_ratio, acc_power,
-    sent, got, redge, ssem, rsem, lsem, esem,
+    sent, got, score_sent, score_got, part_sent, part_got, part_near, redge,
+    ssem, rsem, csem, dsem, psem, qsem, lsem, esem,
 ):
     j = pl.program_id(0)
     repeats, lines, samples = spec.shape[1:]
     chunk = perm.shape[0]
-    tiles, n = sent.shape[:2]
-    rows = redge.shape[1]
+    tiles, n = score_got.shape[:2]
+    half = n // 2
+    rows = redge.shape[2]
     me, t = lax.axis_index("vol"), lax.axis_index("tile")
     other = 1 - t
+    side, place = me // half, me % half
+    here = tile_at(j, tiles)
     part = chunk // CLASSES
     cols = repeats * lines
 
@@ -162,7 +166,7 @@
         1.0,
         0.0,
     )
-    first, last, rated = retina[0, j], retina[1, j], qblock[0, j]
+    first, last, rated = retina[0, here], retina[1, here], qblock[0, here]
     score = jnp.zeros((1, lines), jnp.float32)
     for d in range(NDB):
         ratio, power = acc_ratio[d], acc_power[d]
@@ -178,87 +182,133 @@
         dec, struct = jnp.where(inside, dec, 0.0), jnp.where(inside, struct, 0.0)
         per = DBLK // rows
         for s in range(per):
-            sent[j, d * per + s, :rows, :] = dec[s * rows : (s + 1) * rows]
-            sent[j, d * per + s, rows : 2 * rows, :] = struct[s * rows : (s + 1) * rows]
-    mean = jnp.sum(score, axis=1, keepdims=True) * (1.0 / (DBLK * lines)) + bias[0, j]
-    for u in range(n):
-        sent[j, u, 2 * rows :, :] = jnp.broadcast_to(mean, (8, lines))
-
-    def remote(step, d):
-        target = (me + d) % n
+            u = d * per + s
+            sent[j, u % half, u // half, :rows, :] = dec[s * rows : (s + 1) * rows]
+            sent[j, u % half, u // half, rows:, :] = struct[s * rows : (s + 1) * rows]
+    mean = jnp.sum(score, axis=1, keepdims=True) * (1.0 / (DBLK * lines)) + bias[0, here]
+    score_sent[j] = jnp.broadcast_to(mean, (8, lines))
+
+    def maps(step, d):
+        target = (place + d) % half
         return pltpu.make_async_remote_copy(
-            src_ref=sent.at[step, target], dst_ref=got.at[step, me],
+            src_ref=sent.at[step, target], dst_ref=got.at[step, place],
             send_sem=ssem.at[step, d], recv_sem=rsem.at[step, d],
-            device_id={"vol": target}, device_id_type=MESH,
-        )
-
-    def local(step):
-        return pltpu.make_async_copy(sent.at[step, me], got.at[step, me], lsem.at[step])
+            device_id={"vol": side * half + target}, device_id_type=MESH,
+        )
+
+    def scores(step, d):
+        return pltpu.make_async_remote_copy(
+            src_ref=score_sent.at[step], dst_ref=score_got.at[step, me],
+            send_sem=csem.at[step, d], recv_sem=dsem.at[step, d],
+            device_id={"vol": (me + d) % n}, device_id_type=MESH,
+        )
+
+    def partial(step):
+        return pltpu.make_async_remote_copy(
+            src_ref=part_sent.at[step], dst_ref=part_got.at[step],
+            send_sem=psem.at[step], recv_sem=qsem.at[step],
+            device_id={"vol": (1 - side) * half + place}, device_id_type=MESH,
+        )
+
+    def own_maps(step):
+        return pltpu.make_async_copy(sent.at[step, place], got.at[step, place], lsem.at[0, step])
+
+    def own_score(step):
+        return pltpu.make_async_copy(score_sent.at[step], score_got.at[step, me], lsem.at[1, step])
 
     @pl.when(j == 0)
     def _():
         pl.semaphore_wait(pltpu.get_barrier_semaphore(), n)
 
     for d in range(1, n):
-        remote(j, d).start()
-    local(j).start()
+        scores(j, d).start()
+    for d in range(1, half):
+        maps(j, d).start()
+    own_maps(j).start()
+    own_score(j).start()
 
     @pl.when(j == tiles - 1)
     def _():
-        for step in range(tiles):
-            local(step).wait()
+        lane = lax.broadcasted_iota(jnp.int32, (rows, lines), 1)
+        middle = lines // 2
+        inner = (lane >= middle * t) & (lane < middle + middle * t)
+
+        def arrive(step):
+            own_maps(step).wait()
+            own_score(step).wait()
             for d in range(1, n):
-                remote(step, d).wait_recv()
+                scores(step, d).wait_recv()
+            for d in range(1, half):
+                maps(step, d).wait_recv()
+
+        def add_up(step):
+            ratings = [score_got[step, v, :1, :] for v in range(n)]
+            top = functools.reduce(jnp.maximum, ratings)
+            total = functools.reduce(jnp.add, [jnp.exp(x - top) for x in ratings])
+            weights = [
+                jnp.exp(score_got[step, side * half + v, :1, :] - top) / total
+                for v in range(half)
+            ]
+            for far in range(2):
+                to = 1 - side if far else side
+                ang = square = joined = jnp.zeros((rows, lines), jnp.float32)
+                for v in range(half):
+                    own = got[step, v, to, :rows, :]
+                    if step + 1 < tiles:
+                        after = got[step + 1, v, to, :rows, :]
+                    else:
+                        after = redge[v, to]
+                    before = got[step - 1, v, to, :rows, :] if step else 0.0
+                    wide = jnp.concatenate([own, jnp.where(inner, after, before)], axis=1)
+                    width = 2 * lines
+                    smooth = (
+                        (pltpu.roll(wide, 2, 1) + pltpu.roll(wide, width - 2, 1))[:, :lines]
+                        * (1.0 / 9.0)
+                        + (pltpu.roll(wide, 1, 1) + pltpu.roll(wide, width - 1, 1))[:, :lines]
+                        * (2.0 / 9.0)
+                        + own * (3.0 / 9.0)
+                    )
+                    ws = weights[v] * smooth
+                    ang = ang + ws
+                    square = square + ws * smooth
+                    joined = joined + weights[v] * got[step, v, to, rows:, :]
+                store = part_sent if far else part_near
+                store[step, 0] = ang
+                store[step, 1] = square
+                store[step, 2] = joined
+            partial(step).start()
+
         edge = pltpu.make_async_remote_copy(
-            src_ref=got.at[other * (tiles - 1), :, pl.ds(0, rows), :], dst_ref=redge,
+            src_ref=got.at[tiles - 1, :, :, pl.ds(0, rows), :], dst_ref=redge,
             send_sem=esem.at[0], recv_sem=esem.at[1],
             device_id={"tile": other}, device_id_type=MESH,
         )
-        edge.start()
-        weights = []
+        arrive(0)
         for step in range(tiles):
-            scores = [got[step, v, 2 * rows : 2 * rows + 1, :] for v in range(n)]
-            top = functools.reduce(jnp.maximum, scores)
-            grown = [jnp.exp(x - top) for x in scores]
-            total = functools.reduce(jnp.add, grown)
-            weights.append([x / total for x in grown])
+            if step + 1 < tiles:
+                arrive(step + 1)
+            if step + 1 == max(tiles - 1, 1):
+                edge.start()
+            if step + 1 == tiles:
+                edge.wait_recv()
+            add_up(step)
         for step in range(tiles):
-            at = slice(step * lines, (step + 1) * lines)
-            total = jnp.zeros((rows, lines), jnp.float32)
-            for v in range(n):
-                total = total + weights[step][v] * got[step, v, rows : 2 * rows, :]
-            joined_out[2, :, at] = total
-        lane = lax.broadcasted_iota(jnp.int32, (rows, lines), 1)
-        near = (lane >= t * (lines - 2)) & (lane < 2 + t * lines)
-        width = (tiles + 1) * lines
-        ang = [jnp.zeros((rows, lines), jnp.float32)] * tiles
-        square = list(ang)
-        edge.wait_recv()
-        for v in range(n):
-            wide = jnp.concatenate(
-                [got[step, v, :rows, :] for step in range(tiles)]
-                + [jnp.where(near, redge[v], 0.0)],
-                axis=1,
-            )
-            smooth = (
-                (pltpu.roll(wide, 2, 1) + pltpu.roll(wide, width - 2, 1)) * (1.0 / 9.0)
-                + (pltpu.roll(wide, 1, 1) + pltpu.roll(wide, width - 1, 1)) * (2.0 / 9.0)
-                + wide * (3.0 / 9.0)
-            )
-            for step in range(tiles):
-                w = weights[step][v]
-                s = smooth[:, step * lines : (step + 1) * lines]
-                ws = w * s
-                ang[step] = ang[step] + ws
-                square[step] = square[step] + ws * s
+            partial(step).wait_recv()
+            at = pl.ds(pl.multiple_of(tile_at(step, tiles) * lines, lines), lines)
+            for k in range(3):
+                joined_out[k, :, at] = part_near[step, k] + part_got[step, k]
         for step in range(tiles):
-            at = slice(step * lines, (step + 1) * lines)
-            joined_out[0, :, at] = ang[step]
-            joined_out[1, :, at] = square[step]
-        for step in range(tiles):
+            partial(step).wait_send()
             for d in range(1, n):
-                remote(step, d).wait_send()
+                scores(step, d).wait_send()
+            for d in range(1, half):
+                maps(step, d).wait_send()
         edge.wait_send()
+
+
+def tile_at(step, tiles):
+    t = lax.axis_index("tile")
+    return step + t * (tiles - 1 - 2 * step)
 
 
 def fused(n, spectra, block_scales, retina, qblock, bias):
@@ -275,8 +325,8 @@
         out_shape=jax.ShapeDtypeStruct((3, rows, lines), jnp.float32),
         in_specs=[
             smem, smem, smem,
-            pl.BlockSpec((1, repeats, ABLK, samples), lambda j: (0, 0, j, 0)),
-            pl.BlockSpec((1, repeats, kb, ABLK), lambda j: (0, 0, 0, j)),
+            pl.BlockSpec((1, repeats, ABLK, samples), lambda j: (0, 0, tile_at(j, tiles), 0)),
+            pl.BlockSpec((1, repeats, kb, ABLK), lambda j: (0, 0, 0, tile_at(j, tiles))),
         ],
         out_specs=pl.BlockSpec((3, rows, lines), lambda j: (0, 0, 0)),
         scratch_shapes=[
@@ -287,12 +337,21 @@
             pltpu.VMEM((CLASSES, 2 * ZR, cols), jnp.float32),
             pltpu.VMEM((NDB, ZR, ABLK), jnp.float32),
             pltpu.VMEM((NDB, ZR, ABLK), jnp.float32),
-            pltpu.VMEM((tiles, n, 2 * rows + 8, ABLK), jnp.float32),
-            pltpu.VMEM((tiles, n, 2 * rows + 8, ABLK), jnp.float32),
-            pltpu.VMEM((n, rows, ABLK), jnp.float32),
+            pltpu.VMEM((tiles, n // 2, 2, 2 * rows, ABLK), jnp.float32),
+            pltpu.VMEM((tiles, n // 2, 2, 2 * rows, ABLK), jnp.float32),
+            pltpu.VMEM((tiles, 8, ABLK), jnp.float32),
+            pltpu.VMEM((tiles, n, 8, ABLK), jnp.float32),
+            pltpu.VMEM((tiles, 3, rows, ABLK), jnp.float32),
+            pltpu.VMEM((tiles, 3, rows, ABLK), jnp.float32),
+            pltpu.VMEM((tiles, 3, rows, ABLK), jnp.float32),
+            pltpu.VMEM((n // 2, 2, rows, ABLK), jnp.float32),
+            pltpu.SemaphoreType.DMA((tiles, n // 2)),
+            pltpu.SemaphoreType.DMA((tiles, n // 2)),
             pltpu.SemaphoreType.DMA((tiles, n)),
             pltpu.SemaphoreType.DMA((tiles, n)),
             pltpu.SemaphoreType.DMA((tiles,)),
+            pltpu.SemaphoreType.DMA((tiles,)),
+            pltpu.SemaphoreType.DMA((2, tiles)),
             pltpu.SemaphoreType.DMA((2,)),
         ],
         compiler_params=pltpu.CompilerParams(

time: 55.2 us -> 50.3 us (0.911)
  the two profiles are of different devices: /device:TPU:13 before, /device:TPU:0 now
where the time goes in v4:
time: 50.3 us; the launch traced here: 50.1 us
  Pallas kernels  49.5 us (98%)
  between operations  0.64 us (1%)
    pallas_call x1, Pallas kernels, fused(): pl.pallas_call(fused_kernel, grid=(tiles,), out_shape=jax.ShapeDtypeStruc...  47.8 us
    pallas_call x1, Pallas kernels, finish(): return pl.pallas_call(finish_kernel, out_shape=(out, out, out))(joined)  1.67 us

profile of v4, /device:TPU:0, one launch (start us, length us, event | category | flops | bytes accessed | tf_op | source)
XLA Modules:
  0.0 50.1 jit_solution(867361865079566772)
XLA Ops:
  0.6 47.8 %shard_map.76.joined = f32[3,64,384]{2,1,0:T(8,128)} custom-call(s32[2,3]{1,0:T(2,128)} %bitcast.3, s32[1,3]{1,0:T(1,128)} %qblock.1, f32[1,3]{1,0:T(1,128)} %bias.1, bf16[1,4,384,2048]{3,2,1,0:T(8,128)(2,1)} %spec.1, f32[1,4,16,384]{3,2,1,0:T(8,128)} %bitcast.2), custom_call_target="tpu_custom_call" | custom-call | tf_op jit(solution)/shard_map/pallas_call | solution.py:322
  48.4 1.7 %shard_map.77 = (f32[64,384]{1,0:T(8,128)}, f32[64,384]{1,0:T(8,128)}, f32[64,384]{1,0:T(8,128)}) custom-call(f32[3,64,384]{2,1,0:T(8,128)} %shard_map.76.joined), custom_call_target="tpu_custom_call" | custom-call | tf_op jit(solution)/shard_map/pallas_call | solution.py:372

commit v5 on v4

--- a/solution.py
+++ b/solution.py
@@ -119,18 +119,18 @@
 
     buffers = (ga, gb)
 
-    def multiply(b):
-        for k0 in range(CLASSES):
+    def multiply(b, classes):
+        for k0 in classes:
             buffers[b % 2][k0] = jnp.dot(
                 table[k0, b * 2 * ZR : (b + 1) * 2 * ZR, :],
                 data[k0],
                 preferred_element_type=jnp.float32,
             )
 
-    def reduce(b):
+    def reduce(b, groups):
         g = buffers[b % 2]
 
-        for i in range(ZR // 8):
+        for i in groups:
             at = i * 8
             powers = []
             for r in range(repeats):
@@ -153,11 +153,13 @@
                 acc_power[d, at : at + 8, :] = total
                 acc_ratio[d, at : at + 8, :] = ratio
 
-    multiply(0)
+    multiply(0, range(CLASSES))
+    groups = ZR // 8
     for b in range(BANDS):
-        if b + 1 < BANDS:
-            multiply(b + 1)
-        reduce(b)
+        for k0 in range(CLASSES):
+            if b + 1 < BANDS:
+                multiply(b + 1, (k0,))
+            reduce(b, range(k0 * groups // CLASSES, (k0 + 1) * groups // CLASSES))
 
     flip = jnp.where(
         lax.broadcasted_iota(jnp.int32, (DBLK, ZR), 0)
@@ -259,13 +261,14 @@
                     else:
                         after = redge[v, to]
                     before = got[step - 1, v, to, :rows, :] if step else 0.0
-                    wide = jnp.concatenate([own, jnp.where(inner, after, before)], axis=1)
-                    width = 2 * lines
+                    near = jnp.where(inner, after, before)
+                    right2 = pltpu.roll(jnp.where(lane >= lines - 2, near, own), 2, 1)
+                    right1 = pltpu.roll(jnp.where(lane >= lines - 1, near, own), 1, 1)
+                    left1 = pltpu.roll(jnp.where(lane < 1, near, own), lines - 1, 1)
+                    left2 = pltpu.roll(jnp.where(lane < 2, near, own), lines - 2, 1)
                     smooth = (
-                        (pltpu.roll(wide, 2, 1) + pltpu.roll(wide, width - 2, 1))[:, :lines]
-                        * (1.0 / 9.0)
-                        + (pltpu.roll(wide, 1, 1) + pltpu.roll(wide, width - 1, 1))[:, :lines]
-                        * (2.0 / 9.0)
+                        (right2 + left2) * (1.0 / 9.0)
+                        + (right1 + left1) * (2.0 / 9.0)
                         + own * (3.0 / 9.0)
                     )
                     ws = weights[v] * smooth

time: 50.3 us -> 50.2 us (level)
  no operation moved by 1% of the time
where the time goes in v5:
time: 50.2 us; the launch traced here: 50.1 us
  Pallas kernels  49.4 us (98%)
  between operations  0.64 us (1%)
    pallas_call x1, Pallas kernels, fused(): pl.pallas_call(fused_kernel, grid=(tiles,), out_shape=jax.ShapeDtypeStruc...  47.7 us
    pallas_call x1, Pallas kernels, finish(): return pl.pallas_call(finish_kernel, out_shape=(out, out, out))(joined)  1.67 us

profile of v5, /device:TPU:0, one launch (start us, length us, event | category | flops | bytes accessed | tf_op | source)
XLA Modules:
  0.0 50.1 jit_solution(14853203450378930727)
XLA Ops:
  0.6 47.7 %shard_map.76.joined = f32[3,64,384]{2,1,0:T(8,128)} custom-call(s32[2,3]{1,0:T(2,128)} %bitcast.3, s32[1,3]{1,0:T(1,128)} %qblock.1, f32[1,3]{1,0:T(1,128)} %bias.1, bf16[1,4,384,2048]{3,2,1,0:T(8,128)(2,1)} %spec.1, f32[1,4,16,384]{3,2,1,0:T(8,128)} %bitcast.2), custom_call_target="tpu_custom_call" | custom-call | tf_op jit(solution)/shard_map/pallas_call | solution.py:325
  48.4 1.7 %shard_map.77 = (f32[64,384]{1,0:T(8,128)}, f32[64,384]{1,0:T(8,128)}, f32[64,384]{1,0:T(8,128)}) custom-call(f32[3,64,384]{2,1,0:T(8,128)} %shard_map.76.joined), custom_call_target="tpu_custom_call" | custom-call | tf_op jit(solution)/shard_map/pallas_call | solution.py:375
